TPU v7x, 32 devices: a whole 2x2x4 slice. The times are simulated.
32 devices in a mesh: groups: 2 (over y), row: 4 (over x, core), col: 4 (over z).
Axes of the slice: x: 2, y: 2, z: 4, core: 2. Of those that a mesh axis runs over, the one named last changes fastest.
Arguments:
- queries: bfloat16 [2048, 384], P(('groups', 'row', 'col')), parts along dimension 0, may hold values from -90 to 90
- keys: bfloat16 [2048, 384], P(('groups', 'col', 'row')), parts along dimension 0, may hold values from -15 to 15
- values: bfloat16 [2048, 384], P(('groups', 'col', 'row')), parts along dimension 0, may hold values from -6 to 6
- block_mask: int32 [16, 8], P(('groups', 'row'), 'col'), parts along dimension 0, may hold values from 0 to 1, as said below
- out_weight: bfloat16 [384, 2560], P(None, ('row', 'col')), may hold values from -0.3125 to 0.3125
- residual: bfloat16 [2048, 2560], P(('groups', 'row', 'col')), parts along dimension 0, may hold values from -1.5 to 1.5
Outputs:
- block_out: bfloat16 [2048, 2560], P(('groups', 'row', 'col')), parts along dimension 0
There are 2 independent parts, one for each index of `groups`. A program takes and returns all parts, laid end to end along the dimension named above; an argument that names none is the same for every part. Nothing has to cross between parts.
Inputs may be any that keep to these rules, and one draw needn't show every extreme that they name: Entries are 0 or 1; block_mask[b, b] = 1 for every b. Each query block keeps between 1 and 2 key blocks in each key tile of 2 blocks, and in every pair of a query tile of 2 blocks and a key tile some query block keeps exactly 2.
All inputs are finite; a program needn't handle non-finite values.
Results may differ from a plain program's by a relative error of at most 0.0035.
Values may be sent and summed in bfloat16 or wider, within the bound.
A program may use at most 64 MiB of HBM per device.

v0:
```python
import functools
import math

import jax
import jax.numpy as jnp
from jax import lax
from jax.experimental import pallas as pl
from jax.experimental.pallas import tpu as pltpu
from jax.sharding import PartitionSpec as P

HD = 128
HEADS = 3
BLK = 128
MESH = pl.DeviceIdType.MESH


def local(queries, keys, values, block_mask, out_weight, residual):
    score_scale = 1.0 / math.sqrt(HD)
    query_tile = lax.all_gather(queries, "col", axis=0, tiled=True)
    key_tile, value_tile = (
        lax.all_gather(keys, "row", axis=0, tiled=True),
        lax.all_gather(values, "row", axis=0, tiled=True),
    )
    query_count = block_mask.shape[0]
    key_count = block_mask.shape[1]
    keep_most = max(2, 7 * key_count // 16)
    if query_count % 4 == 0:
        group_size = 4
    elif query_count % 2 == 0:
        group_size = 2
    else:
        group_size = 1
    key_blocks = key_tile.reshape(key_count, BLK, HEADS, HD)
    value_blocks = value_tile.reshape(key_count, BLK, HEADS, HD)
    within = jnp.arange(key_count, dtype=jnp.int32)
    priority = block_mask * (2 * key_count) + (key_count - within)[None, :]
    top_values, chosen = lax.top_k(priority, keep_most)
    usable = jnp.take_along_axis(block_mask, chosen, axis=1) > 0
    steps_count = query_count // group_size
    query_groups = query_tile.reshape(steps_count, group_size, BLK, HEADS, HD)
    chosen_groups = chosen.reshape(steps_count, group_size, keep_most)
    usable_groups = usable.reshape(steps_count, group_size, keep_most)

    def one_step(operands):
        query_rows, picked, allowed = operands
        near_keys = key_blocks[picked]
        near_values = value_blocks[picked]
        scores = (
            jnp.einsum(
                "gqhd,gkbhd->gqhkb", query_rows, near_keys, preferred_element_type=jnp.float32
            )
            * score_scale
        )
        scores = jnp.where(allowed[:, None, None, :, None], scores, -jnp.inf)
        tile_max = jnp.max(scores, axis=(3, 4))
        weights = jnp.exp(scores - tile_max[:, :, :, None, None])
        tile_total = jnp.sum(weights, axis=(3, 4))
        rounded = weights.astype(jnp.bfloat16)
        tile_sum = jnp.einsum(
            "gqhkb,gkbhd->gqhd", rounded, near_values, preferred_element_type=jnp.float32
        )
        return (tile_sum, tile_max, tile_total)

    tile_sum, tile_max, tile_total = lax.map(one_step, (query_groups, chosen_groups, usable_groups))
    query_rows_all = query_count * BLK
    tile_sum = tile_sum.reshape(query_rows_all, HEADS, HD)
    tile_max = tile_max.reshape(query_rows_all, HEADS)
    tile_total = tile_total.reshape(query_rows_all, HEADS)
    col_count = lax.axis_size("col")
    own_rows = query_rows_all // col_count
    moved_sum, moved_max, moved_total = (
        lax.all_to_all(
            tile_sum.reshape(col_count, own_rows, HEADS * HD),
            "col",
            split_axis=0,
            concat_axis=0,
            tiled=True,
        ),
        lax.all_to_all(
            tile_max.reshape(col_count, own_rows, HEADS),
            "col",
            split_axis=0,
            concat_axis=0,
            tiled=True,
        ),
        lax.all_to_all(
            tile_total.reshape(col_count, own_rows, HEADS),
            "col",
            split_axis=0,
            concat_axis=0,
            tiled=True,
        ),
    )
    row_max = jnp.max(moved_max, axis=0)
    factor = jnp.exp(moved_max - row_max[None, :, :])
    numer = jnp.sum(
        moved_sum.reshape(col_count, own_rows, HEADS, HD) * factor[:, :, :, None], axis=0
    )
    denom = jnp.sum(moved_total * factor, axis=0)
    attended = (numer / denom[:, :, None]).reshape(own_rows, HEADS * HD).astype(jnp.bfloat16)
    projected = jnp.dot(
        attended,
        lax.all_gather(out_weight, ("row", "col"), axis=1, tiled=True),
        preferred_element_type=jnp.float32,
    )
    return (projected + residual.astype(jnp.float32)).astype(jnp.bfloat16)


def fused_kernel(
    rows, cols, q_in, k_in, v_in, mask_in, w_in, res_in, out_ref,
    qbuf, kv, wt, mask, psend, precv, ssend, srecv,
    osum, res, load_sem, send_sem, recv_sem,
):
    score_scale = 1.0 / math.sqrt(HD)
    g = lax.axis_index("groups")
    r = lax.axis_index("row")
    c = lax.axis_index("col")
    r_chip = lax.rem(r + 2, rows)
    r_core = r + 1 - 2 * lax.rem(r, 2)
    r_both = r_chip + 1 - 2 * lax.rem(r, 2)
    other = 1 - g
    chip = {"row": r_chip}
    core = {"row": r_core}
    video = {"groups": other}
    diagonal = {"groups": other, "row": r_chip}

    loads = [
        pltpu.make_async_copy(q_in, qbuf.at[c], load_sem.at[0]),
        pltpu.make_async_copy(k_in, kv.at[r, 0], load_sem.at[1]),
        pltpu.make_async_copy(v_in, kv.at[r, 1], load_sem.at[2]),
        pltpu.make_async_copy(w_in, wt.at[r, c], load_sem.at[3]),
        pltpu.make_async_copy(mask_in, mask, load_sem.at[4]),
        pltpu.make_async_copy(res_in, res, load_sem.at[5]),
    ]
    for load in loads:
        load.start()

    barrier = pltpu.get_barrier_semaphore()
    peers = [{"col": lax.rem(c + j, cols)} for j in range(1, cols)] + [chip, core, video, diagonal]
    for peer in peers:
        pl.semaphore_signal(barrier, inc=1, device_id=peer, device_id_type=MESH)
    pl.semaphore_wait(barrier, len(peers))

    started = []

    def send(src, dst, device):
        index = len(started)
        copy = pltpu.make_async_remote_copy(
            src_ref=src, dst_ref=dst,
            send_sem=send_sem.at[index], recv_sem=recv_sem.at[index],
            device_id=device, device_id_type=MESH,
        )
        copy.start()
        started.append(copy)
        return copy

    pair = c + 1 - 2 * lax.rem(c, 2)
    across = lax.rem(c + 2, cols)
    far = lax.rem(pair + 2, cols)
    targets = [far, across, pair]
    arriving = []
    to_core = []

    def spread(u, direct=True):
        unit = wt.at[r, u, g]
        if direct:
            arriving.append((wt.at[r_chip, u, other], send(unit, unit, diagonal)))
        arriving.append((wt.at[r_chip, u, g], send(unit, unit, chip)))
        arriving.append((wt.at[r, u, other], send(unit, unit, video)))
        to_core.append(send(unit, unit, core))

    loads[3].wait()
    across_copy = send(wt.at[r, c, g], wt.at[r, c, g], {"col": across})
    pair_copy = send(wt.at[r, c, g], wt.at[r, c, g], {"col": pair})
    loads[0].wait()
    q_copies = [send(qbuf.at[c], qbuf.at[c], {"col": t}) for t in targets]
    loads[1].wait()
    loads[2].wait()
    kv_chip = send(kv.at[r], kv.at[r], chip)
    kv_core = send(kv.at[r], kv.at[r], core)

    half = wt.shape[3]
    own_core = send(wt.at[r, c], wt.at[r, c], core)
    to_core.append(own_core)

    kv_chip.wait_recv()
    kv_both = send(kv.at[r_chip], kv.at[r_chip], core)
    across_copy.wait_recv()
    far_copy = send(wt.at[r, across, g], wt.at[r, across, g], {"col": pair})
    spread(across, direct=False)
    own_chip = send(wt.at[r, c], wt.at[r, c], chip)
    loads[4].wait()
    kv_core.wait_recv()
    kv_both.wait_recv()
    pair_copy.wait_recv()
    spread(pair)
    for copy in q_copies:
        copy.wait_recv()

    own = qbuf.shape[1]
    key_count = mask.shape[1]
    query_count = mask.shape[0]
    for h in range(HEADS):
        lanes = slice(h * HD, (h + 1) * HD)
        key_rows = kv[:, 0, :, lanes].reshape(-1, HD)
        value_rows = kv[:, 1, :, lanes].reshape(-1, HD)
        query_rows = qbuf[:, :, lanes].reshape(-1, HD)
        scores = lax.dot_general(
            key_rows, query_rows, (((1,), (1,)), ((), ())), preferred_element_type=jnp.float32
        )
        scores = scores * score_scale
        seen = jnp.concatenate(
            [
                jnp.concatenate(
                    [
                        jnp.broadcast_to(mask[i : i + 1, j : j + 1], (BLK, BLK))
                        for i in range(query_count)
                    ],
                    axis=1,
                )
                for j in range(key_count)
            ],
            axis=0,
        )
        scores = jnp.where(seen > 0, scores, -jnp.inf)
        tile_max = jnp.max(scores, axis=0, keepdims=True)
        weights = jnp.exp(scores - tile_max)
        tile_total = jnp.sum(weights, axis=0, keepdims=True)
        tile_sum = lax.dot_general(
            weights.astype(jnp.bfloat16), value_rows, (((0,), (0,)), ((), ())),
            preferred_element_type=jnp.float32,
        )
        for i in range(cols):
            part = slice(i * own, (i + 1) * own)
            osum[i, :, lanes] = tile_sum[part]
            psend[i, :, lanes] = tile_sum[part].astype(jnp.bfloat16)
            ssend[i, h : h + 1, 0:own] = tile_max[:, part]
            ssend[i, HEADS + h : HEADS + h + 1, 0:own] = tile_total[:, part]
    p_copies = [send(psend.at[t], precv.at[c], {"col": t}) for t in targets]
    s_copies = [send(ssend.at[t], srecv.at[c], {"col": t}) for t in targets]
    precv[c] = psend[c]
    srecv[c] = ssend[c]

    far_copy.wait_recv()
    spread(far)
    unit, copy = arriving.pop(0)
    copy.wait_recv()
    to_core.append(send(unit, unit, core))
    arriving.append((wt.at[r_chip, across, other], send(unit, unit, video)))
    own_chip.wait_recv()
    to_core.append(send(wt.at[r_chip, c], wt.at[r_chip, c], core))
    for unit, copy in arriving:
        copy.wait_recv()
        to_core.append(send(unit, unit, core))

    for copy in s_copies + p_copies:
        copy.wait_recv()
    stats = [srecv[t] for t in range(cols)]
    maxes = [s[0:HEADS, :] for s in stats]
    totals = [s[HEADS : 2 * HEADS, :] for s in stats]
    row_max = functools.reduce(jnp.maximum, maxes)
    factors = [jnp.exp(m - row_max) for m in maxes]
    denom = functools.reduce(jnp.add, [t * f for t, f in zip(totals, factors)])
    own_factor = jnp.exp(ssend[c, 0:HEADS, :] - row_max)
    low = osum[c] - psend[c].astype(jnp.float32)
    pad = [jnp.zeros((8 - HEADS, denom.shape[1]), jnp.float32)]
    spread = jnp.concatenate(
        [x for f in factors + [denom, own_factor] for x in [f] + pad], axis=0
    )
    fill = jnp.zeros((spread.shape[1] - spread.shape[0], spread.shape[1]), jnp.float32)
    spread = jnp.concatenate([spread, fill], axis=0).T[0:own]
    attended = []
    for h in range(HEADS):
        lanes = slice(h * HD, (h + 1) * HD)
        numer = functools.reduce(
            jnp.add,
            [
                precv[t, :, lanes].astype(jnp.float32) * spread[:, 8 * t + h : 8 * t + h + 1]
                for t in range(cols)
            ],
        )
        numer += low[:, lanes] * spread[:, 8 * cols + 8 + h : 8 * cols + 9 + h]
        attended.append(numer / spread[:, 8 * cols + h : 8 * cols + h + 1])
    attended = jnp.concatenate(attended, axis=1).astype(jnp.bfloat16)

    width = cols * 2 * half

    def project(row):
        columns = pl.ds(pl.multiple_of(row * width, BLK), width)
        projected = lax.dot_general(
            attended, wt[row].reshape(width, HEADS * HD), (((1,), (1,)), ((), ())),
            preferred_element_type=jnp.float32,
        )
        total = projected + res[:, columns].astype(jnp.float32)
        out_ref[:, columns] = total.astype(jnp.bfloat16)

    loads[5].wait()
    project(r)
    project(r_chip)
    for copy in to_core:
        copy.wait_recv()
    project(r_core)
    project(r_both)
    for copy in started:
        copy.wait_send()


def fused(queries, keys, values, block_mask, out_weight, residual):
    rows, cols = lax.axis_size("row"), lax.axis_size("col")
    own, width = queries.shape
    depth, part = out_weight.shape
    copies = 5 * (cols - 1) + 40 + 8 * cols
    any_space = pl.BlockSpec(memory_space=pl.ANY)
    projected = pl.pallas_call(
        functools.partial(fused_kernel, rows, cols),
        out_shape=jax.ShapeDtypeStruct((own, residual.shape[1]), jnp.bfloat16),
        in_specs=[any_space] * 6,
        out_specs=pl.BlockSpec(memory_space=pltpu.VMEM),
        scratch_shapes=[
            pltpu.VMEM((cols, own, width), jnp.bfloat16),
            pltpu.VMEM((rows, 2, own, width), jnp.bfloat16),
            pltpu.VMEM((rows, cols, 2, part // 2, depth), jnp.bfloat16),
            pltpu.VMEM(block_mask.shape, jnp.int32),
            pltpu.VMEM((cols, own, width), jnp.bfloat16),
            pltpu.VMEM((cols, own, width), jnp.bfloat16),
            pltpu.VMEM((cols, 8, BLK), jnp.float32),
            pltpu.VMEM((cols, 8, BLK), jnp.float32),
            pltpu.VMEM((cols, own, width), jnp.float32),
            pltpu.VMEM(residual.shape, jnp.bfloat16),
            pltpu.SemaphoreType.DMA((6,)),
            pltpu.SemaphoreType.DMA((copies,)),
            pltpu.SemaphoreType.DMA((copies,)),
        ],
        compiler_params=pltpu.CompilerParams(collective_id=0, has_side_effects=True),
    )(queries, keys, values, block_mask, out_weight.T.reshape(2, part // 2, depth), residual)
    return projected


def kernel_fits(mesh):
    return mesh.shape["groups"] == 2 and mesh.shape["row"] == 4 and mesh.shape["col"] == 4


def solution(mesh):
    body = fused if kernel_fits(mesh) else local
    placed = (
        P(("groups", "row", "col"), None),
        P(("groups", "col", "row"), None),
        P(("groups", "col", "row"), None),
        P(("groups", "row"), "col"),
        P(None, ("row", "col")),
        P(("groups", "row", "col"), None),
    )
    return jax.shard_map(
        body,
        mesh=mesh,
        in_specs=placed,
        out_specs=P(("groups", "row", "col"), None),
        check_vma=False,
    )
```

profile of v0, /device:TPU:1, one launch (start us, length us, event | category | flops | bytes accessed | tf_op | source)
XLA Modules:
  0.0 25.7 jit_solution(7222353386626039243)
XLA Ops:
  0.0 23.9 %shard_map.64 = bf16[64,2560]{1,0:T(8,128)(2,1)} custom-call(bf16[64,384]{1,0:T(8,128)(2,1)} %q_in.1, bf16[64,384]{1,0:T(8,128)(2,1)} %k_in.1, bf16[64,384]{1,0:T(8,128)(2,1)} %v_in.1, s32[2,2]{1,0:T(2,128)} %mask_in.1, bf16[2,80,384]{2,1,0:T(8,128)(2,1)} %bitcast.3, bf16[64,2560]{1,0:T(8,128)(2,1)} %res_in.1), custom_call_target="tpu_custom_call" | custom-call | tf_op jit(solution)/shard_map/pallas_call | solution.py:314
  23.9 1.7 %copy.8 = bf16[64,2560]{1,0:T(8,128)(2,1)} copy(bf16[64,2560]{1,0:T(8,128)(2,1)} %shard_map.64) | data formatting | bytes 655360
where the time goes:
time: 25.8 us; the launch traced here: 25.7 us
  Pallas kernels  23.9 us (93%)
  local copies, waits for them, and re-layouts  1.72 us (7%)
    pallas_call x1, Pallas kernels, fused(): pl.pallas_call(functools.partial(fused_kernel, rows, cols), out_shape=jax...  23.9 us
    unnamed x1, local copies, waits for them, and re-layouts  1.72 us

commit v1 on v0

--- a/solution.py
+++ b/solution.py
@@ -313,7 +313,7 @@
     any_space = pl.BlockSpec(memory_space=pl.ANY)
     projected = pl.pallas_call(
         functools.partial(fused_kernel, rows, cols),
-        out_shape=jax.ShapeDtypeStruct((own, residual.shape[1]), jnp.bfloat16),
+        out_shape=pltpu.VMEM((own, residual.shape[1]), jnp.bfloat16),
         in_specs=[any_space] * 6,
         out_specs=pl.BlockSpec(memory_space=pltpu.VMEM),
         scratch_shapes=[

time: 25.8 us -> 24.1 us (0.934)
  local copies, waits for them, and re-layouts: 1.72 us -> 0.73 us
  Pallas kernels: 23.9 us -> 23.2 us
    unnamed x1, local copies, waits for them, and re-layouts: 1.72 us -> 0.73 us
    pallas_call x1, Pallas kernels: 23.9 us -> 23.2 us  [fused(): pl.pallas_call(functools.partial(fused_kernel, rows, cols), out_shape=plt...]
where the time goes in v1:
time: 24.1 us; the launch traced here: 24 us
  Pallas kernels  23.2 us (96%)
  local copies, waits for them, and re-layouts  0.73 us (3%)
    pallas_call x1, Pallas kernels, fused(): pl.pallas_call(functools.partial(fused_kernel, rows, cols), out_shape=plt...  23.2 us
    unnamed x1, local copies, waits for them, and re-layouts  0.73 us

profile of v1, /device:TPU:1, one launch (start us, length us, event | category | flops | bytes accessed | tf_op | source)
XLA Modules:
  0.0 24.0 jit_solution(9281843038530706741)
XLA Ops:
  0.0 23.2 %shard_map.64 = bf16[64,2560]{1,0:T(8,128)(2,1)S(1)} custom-call(bf16[64,384]{1,0:T(8,128)(2,1)} %q_in.1, bf16[64,384]{1,0:T(8,128)(2,1)} %k_in.1, bf16[64,384]{1,0:T(8,128)(2,1)} %v_in.1, s32[2,2]{1,0:T(2,128)} %mask_in.1, bf16[2,80,384]{2,1,0:T(8,128)(2,1)} %bitcast.3, bf16[64,2560]{1,0:T(8,128)(2,1)} %res_in.1), custom_call_target="tpu_custom_call" | custom-call | tf_op jit(solution)/shard_map/pallas_call | solution.py:314
  23.2 0.7 %copy.8 = bf16[64,2560]{1,0:T(8,128)(2,1)} copy(bf16[64,2560]{1,0:T(8,128)(2,1)S(1)} %shard_map.64) | data formatting | bytes 655360

commit v2 on v1

v2 whole, which is shorter than its diff:
```python
import functools
import math

import jax
import jax.numpy as jnp
from jax import lax
from jax.experimental import pallas as pl
from jax.experimental.pallas import tpu as pltpu
from jax.sharding import PartitionSpec as P

HD = 128
HEADS = 3
BLK = 128
MESH = pl.DeviceIdType.MESH


def local(queries, keys, values, block_mask, out_weight, residual):
    score_scale = 1.0 / math.sqrt(HD)
    query_tile = lax.all_gather(queries, "col", axis=0, tiled=True)
    key_tile, value_tile = (
        lax.all_gather(keys, "row", axis=0, tiled=True),
        lax.all_gather(values, "row", axis=0, tiled=True),
    )
    query_count = block_mask.shape[0]
    key_count = block_mask.shape[1]
    keep_most = max(2, 7 * key_count // 16)
    if query_count % 4 == 0:
        group_size = 4
    elif query_count % 2 == 0:
        group_size = 2
    else:
        group_size = 1
    key_blocks = key_tile.reshape(key_count, BLK, HEADS, HD)
    value_blocks = value_tile.reshape(key_count, BLK, HEADS, HD)
    within = jnp.arange(key_count, dtype=jnp.int32)
    priority = block_mask * (2 * key_count) + (key_count - within)[None, :]
    top_values, chosen = lax.top_k(priority, keep_most)
    usable = jnp.take_along_axis(block_mask, chosen, axis=1) > 0
    steps_count = query_count // group_size
    query_groups = query_tile.reshape(steps_count, group_size, BLK, HEADS, HD)
    chosen_groups = chosen.reshape(steps_count, group_size, keep_most)
    usable_groups = usable.reshape(steps_count, group_size, keep_most)

    def one_step(operands):
        query_rows, picked, allowed = operands
        near_keys = key_blocks[picked]
        near_values = value_blocks[picked]
        scores = (
            jnp.einsum(
                "gqhd,gkbhd->gqhkb", query_rows, near_keys, preferred_element_type=jnp.float32
            )
            * score_scale
        )
        scores = jnp.where(allowed[:, None, None, :, None], scores, -jnp.inf)
        tile_max = jnp.max(scores, axis=(3, 4))
        weights = jnp.exp(scores - tile_max[:, :, :, None, None])
        tile_total = jnp.sum(weights, axis=(3, 4))
        rounded = weights.astype(jnp.bfloat16)
        tile_sum = jnp.einsum(
            "gqhkb,gkbhd->gqhd", rounded, near_values, preferred_element_type=jnp.float32
        )
        return (tile_sum, tile_max, tile_total)

    tile_sum, tile_max, tile_total = lax.map(one_step, (query_groups, chosen_groups, usable_groups))
    query_rows_all = query_count * BLK
    tile_sum = tile_sum.reshape(query_rows_all, HEADS, HD)
    tile_max = tile_max.reshape(query_rows_all, HEADS)
    tile_total = tile_total.reshape(query_rows_all, HEADS)
    col_count = lax.axis_size("col")
    own_rows = query_rows_all // col_count
    moved_sum, moved_max, moved_total = (
        lax.all_to_all(
            tile_sum.reshape(col_count, own_rows, HEADS * HD),
            "col",
            split_axis=0,
            concat_axis=0,
            tiled=True,
        ),
        lax.all_to_all(
            tile_max.reshape(col_count, own_rows, HEADS),
            "col",
            split_axis=0,
            concat_axis=0,
            tiled=True,
        ),
        lax.all_to_all(
            tile_total.reshape(col_count, own_rows, HEADS),
            "col",
            split_axis=0,
            concat_axis=0,
            tiled=True,
        ),
    )
    row_max = jnp.max(moved_max, axis=0)
    factor = jnp.exp(moved_max - row_max[None, :, :])
    numer = jnp.sum(
        moved_sum.reshape(col_count, own_rows, HEADS, HD) * factor[:, :, :, None], axis=0
    )
    denom = jnp.sum(moved_total * factor, axis=0)
    attended = (numer / denom[:, :, None]).reshape(own_rows, HEADS * HD).astype(jnp.bfloat16)
    projected = jnp.dot(
        attended,
        lax.all_gather(out_weight, ("row", "col"), axis=1, tiled=True),
        preferred_element_type=jnp.float32,
    )
    return (projected + residual.astype(jnp.float32)).astype(jnp.bfloat16)


def fused_kernel(
    slots, q_in, k_in, v_in, mask_in, w_in, res_in, out_ref,
    qbuf, kv, wt, mask, psend, precv, ssend, srecv,
    osum, res, blank, load_sem, send_sem, recv_sem,
):
    score_scale = 1.0 / math.sqrt(HD)
    g = lax.axis_index("groups")
    r = lax.axis_index("row")
    c = lax.axis_index("col")
    rows, cols = wt.shape[0], wt.shape[1]
    r_chip = lax.rem(r + 2, rows)
    r_core = r + 1 - 2 * lax.rem(r, 2)
    r_both = r_chip + 1 - 2 * lax.rem(r, 2)
    other = 1 - g
    chip = {"row": r_chip}
    core = {"row": r_core}
    video = {"groups": other}
    diagonal = {"groups": other, "row": r_chip}

    loads = [
        pltpu.make_async_copy(q_in, qbuf.at[c], load_sem.at[0]),
        pltpu.make_async_copy(k_in, kv.at[r, 0], load_sem.at[1]),
        pltpu.make_async_copy(v_in, kv.at[r, 1], load_sem.at[2]),
        pltpu.make_async_copy(w_in, wt.at[r, c], load_sem.at[3]),
        pltpu.make_async_copy(mask_in, mask, load_sem.at[4]),
        pltpu.make_async_copy(res_in, res, load_sem.at[5]),
    ]
    for load in loads:
        load.start()

    barrier = pltpu.get_barrier_semaphore()
    peers = [{"col": lax.rem(c + j, cols)} for j in range(1, cols)] + [chip, core, video, diagonal]
    for peer in peers:
        pl.semaphore_signal(barrier, inc=1, device_id=peer, device_id_type=MESH)
    pl.semaphore_wait(barrier, len(peers))

    bytes_of = {}
    names = []

    def send(src, dst, device, name):
        if name not in bytes_of:
            names.append(name)
            bytes_of[name] = 0
        size = math.prod(dst.shape) * dst.dtype.itemsize
        bytes_of[name] += size
        bytes_of[""] = bytes_of.get("", 0) + size
        pltpu.make_async_remote_copy(
            src_ref=src, dst_ref=dst,
            send_sem=send_sem, recv_sem=recv_sem.at[names.index(name)],
            device_id=device, device_id_type=MESH,
        ).start()

    def settle(sem, size):
        view = blank.at[pl.ds(0, size // (2 * BLK)), :]
        pltpu.make_async_copy(view, view, sem).wait()

    def wait(name):
        settle(recv_sem.at[names.index(name)], bytes_of[name])

    pair = c + 1 - 2 * lax.rem(c, 2)
    across = lax.rem(c + 2, cols)
    far = lax.rem(pair + 2, cols)
    targets = [far, across, pair]

    def spread(u, name, direct=True):
        unit = wt.at[r, u, g]
        if direct:
            send(unit, unit, diagonal, name + "_d")
        send(unit, unit, chip, name + "_x")
        send(unit, unit, video, name + "_y")
        send(unit, unit, core, "core_r")

    def relay_y(u, name):
        wait(name + "_y")
        unit = wt.at[r, u, other]
        send(unit, unit, core, "core_r")

    def relay_x(u, name, forward=False):
        wait(name + "_x")
        unit = wt.at[r_chip, u, g]
        send(unit, unit, core, "core_x")
        if forward:
            send(unit, unit, video, name + "_d")

    def relay_d(u, name):
        wait(name + "_d")
        unit = wt.at[r_chip, u, other]
        send(unit, unit, core, "core_x")

    own = qbuf.shape[1]
    key_count = mask.shape[1]
    query_count = mask.shape[0]
    attended = []

    def attend():
        for h in range(HEADS):
            lanes = slice(h * HD, (h + 1) * HD)
            key_rows = kv[:, 0, :, lanes].reshape(-1, HD)
            value_rows = kv[:, 1, :, lanes].reshape(-1, HD)
            query_rows = qbuf[:, :, lanes].reshape(-1, HD)
            scores = lax.dot_general(
                key_rows, query_rows, (((1,), (1,)), ((), ())), preferred_element_type=jnp.float32
            )
            scores = scores * score_scale
            seen = jnp.concatenate(
                [
                    jnp.concatenate(
                        [
                            jnp.broadcast_to(mask[i : i + 1, j : j + 1], (BLK, BLK))
                            for i in range(query_count)
                        ],
                        axis=1,
                    )
                    for j in range(key_count)
                ],
                axis=0,
            )
            scores = jnp.where(seen > 0, scores, -jnp.inf)
            tile_max = jnp.max(scores, axis=0, keepdims=True)
            weights = jnp.exp(scores - tile_max)
            tile_total = jnp.sum(weights, axis=0, keepdims=True)
            tile_sum = lax.dot_general(
                weights.astype(jnp.bfloat16), value_rows, (((0,), (0,)), ((), ())),
                preferred_element_type=jnp.float32,
            )
            for i in range(cols):
                part = slice(i * own, (i + 1) * own)
                osum[i, :, lanes] = tile_sum[part]
                psend[i, :, lanes] = tile_sum[part].astype(jnp.bfloat16)
                ssend[i, h : h + 1, 0:own] = tile_max[:, part]
                ssend[i, HEADS + h : HEADS + h + 1, 0:own] = tile_total[:, part]
        for t in targets:
            send(ssend.at[t], srecv.at[c], {"col": t}, "p")
            send(psend.at[t], precv.at[c], {"col": t}, "p")
        precv[c] = psend[c]
        srecv[c] = ssend[c]

    def merge():
        wait("p")
        stats = [srecv[t] for t in range(cols)]
        maxes = [s[0:HEADS, :] for s in stats]
        totals = [s[HEADS : 2 * HEADS, :] for s in stats]
        row_max = functools.reduce(jnp.maximum, maxes)
        factors = [jnp.exp(m - row_max) for m in maxes]
        denom = functools.reduce(jnp.add, [t * f for t, f in zip(totals, factors)])
        own_factor = jnp.exp(ssend[c, 0:HEADS, :] - row_max)
        low = osum[c] - psend[c].astype(jnp.float32)
        pad = [jnp.zeros((8 - HEADS, denom.shape[1]), jnp.float32)]
        table = jnp.concatenate(
            [x for f in factors + [denom, own_factor] for x in [f] + pad], axis=0
        )
        fill = jnp.zeros((table.shape[1] - table.shape[0], table.shape[1]), jnp.float32)
        table = jnp.concatenate([table, fill], axis=0).T[0:own]
        heads = []
        for h in range(HEADS):
            lanes = slice(h * HD, (h + 1) * HD)
            numer = functools.reduce(
                jnp.add,
                [
                    precv[t, :, lanes].astype(jnp.float32) * table[:, 8 * t + h : 8 * t + h + 1]
                    for t in range(cols)
                ],
            )
            numer += low[:, lanes] * table[:, 8 * cols + 8 + h : 8 * cols + 9 + h]
            heads.append(numer / table[:, 8 * cols + h : 8 * cols + h + 1])
        attended.append(jnp.concatenate(heads, axis=1).astype(jnp.bfloat16))
        loads[5].wait()

    width = cols * 2 * wt.shape[3]

    def project(row):
        columns = pl.ds(pl.multiple_of(row * width, BLK), width)
        projected = lax.dot_general(
            attended[0], wt[row].reshape(width, HEADS * HD), (((1,), (1,)), ((), ())),
            preferred_element_type=jnp.float32,
        )
        total = projected + res[:, columns].astype(jnp.float32)
        out_ref[:, columns] = total.astype(jnp.bfloat16)

    loads[3].wait()
    send(wt.at[r, c, g], wt.at[r, c, g], {"col": across}, "across")
    send(wt.at[r, c, g], wt.at[r, c, g], {"col": pair}, "pair")
    loads[0].wait()
    for t in targets:
        send(qbuf.at[c], qbuf.at[c], {"col": t}, "q")
    loads[1].wait()
    loads[2].wait()
    send(kv.at[r], kv.at[r], chip, "kv_chip")
    send(kv.at[r], kv.at[r], core, "kv_core")
    send(wt.at[r, c], wt.at[r, c], core, "core_r")
    wait("kv_chip")
    send(kv.at[r_chip], kv.at[r_chip], core, "kv_core")
    wait("across")
    send(wt.at[r, across, g], wt.at[r, across, g], {"col": pair}, "far")
    spread(across, "across", direct=False)
    send(wt.at[r, c], wt.at[r, c], chip, "own_x")
    wait("pair")
    spread(pair, "pair")
    wait("q")
    wait("kv_core")
    loads[4].wait()
    attend()
    wait("far")
    spread(far, "far")
    relay_x(across, "across", forward=True)
    wait("own_x")
    send(wt.at[r_chip, c], wt.at[r_chip, c], core, "core_x")
    relay_y(across, "across")
    relay_x(pair, "pair")
    relay_y(pair, "pair")
    relay_d(pair, "pair")
    relay_x(far, "far")
    relay_y(far, "far")
    relay_d(far, "far")
    relay_d(across, "across")
    merge()
    project(r)
    project(r_chip)
    wait("core_r")
    project(r_core)
    wait("core_x")
    project(r_both)
    assert len(names) == slots, len(names)
    settle(send_sem, bytes_of[""])


def fused(queries, keys, values, block_mask, out_weight, residual):
    rows, cols = lax.axis_size("row"), lax.axis_size("col")
    own, width = queries.shape
    depth, part = out_weight.shape
    slots = 19
    any_space = pl.BlockSpec(memory_space=pl.ANY)
    return pl.pallas_call(
        functools.partial(fused_kernel, slots),
        out_shape=pltpu.VMEM((own, residual.shape[1]), jnp.bfloat16),
        in_specs=[any_space] * 6,
        out_specs=pl.BlockSpec(memory_space=pltpu.VMEM),
        scratch_shapes=[
            pltpu.VMEM((cols, own, width), jnp.bfloat16),
            pltpu.VMEM((rows, 2, own, width), jnp.bfloat16),
            pltpu.VMEM((rows, cols, 2, part // 2, depth), jnp.bfloat16),
            pltpu.VMEM(block_mask.shape, jnp.int32),
            pltpu.VMEM((cols, own, width), jnp.bfloat16),
            pltpu.VMEM((cols, own, width), jnp.bfloat16),
            pltpu.VMEM((cols, 8, BLK), jnp.float32),
            pltpu.VMEM((cols, 8, BLK), jnp.float32),
            pltpu.VMEM((cols, own, width), jnp.float32),
            pltpu.VMEM(residual.shape, jnp.bfloat16),
            pltpu.VMEM((rows * cols * 2 * part * depth // BLK, BLK), jnp.bfloat16),
            pltpu.SemaphoreType.DMA((6,)),
            pltpu.SemaphoreType.DMA,
            pltpu.SemaphoreType.DMA((slots,)),
        ],
        compiler_params=pltpu.CompilerParams(collective_id=0, has_side_effects=True),
    )(queries, keys, values, block_mask, out_weight.T.reshape(2, part // 2, depth), residual)


def kernel_fits(mesh):
    return mesh.shape["groups"] == 2 and mesh.shape["row"] == 4 and mesh.shape["col"] == 4


def solution(mesh):
    body = fused if kernel_fits(mesh) else local
    placed = (
        P(("groups", "row", "col"), None),
        P(("groups", "col", "row"), None),
        P(("groups", "col", "row"), None),
        P(("groups", "row"), "col"),
        P(None, ("row", "col")),
        P(("groups", "row", "col"), None),
    )
    return jax.shard_map(
        body,
        mesh=mesh,
        in_specs=placed,
        out_specs=P(("groups", "row", "col"), None),
        check_vma=False,
    )
```

time: 24.1 us -> 22.6 us (0.938); the launches traced: 24 us -> 22.2 us
  Pallas kernels: 23.2 us -> 21.4 us
    pallas_call x1, Pallas kernels: 23.2 us -> 21.4 us  [fused(): pl.pallas_call(functools.partial(fused_kernel, slots), out_shape=pltpu.VM...]
where the time goes in v2:
time: 22.6 us; the launch traced here: 22.2 us
  Pallas kernels  21.4 us (95%)
  local copies, waits for them, and re-layouts  0.73 us (3%)
    pallas_call x1, Pallas kernels, fused(): pl.pallas_call(functools.partial(fused_kernel, slots), out_shape=pltpu.VM...  21.4 us
    unnamed x1, local copies, waits for them, and re-layouts  0.73 us

profile of v2, /device:TPU:1, one launch (start us, length us, event | category | flops | bytes accessed | tf_op | source)
XLA Modules:
  0.0 22.2 jit_solution(5323331816352529171)
XLA Ops:
  0.0 21.4 %shard_map.64 = bf16[64,2560]{1,0:T(8,128)(2,1)S(1)} custom-call(bf16[64,384]{1,0:T(8,128)(2,1)} %q_in.1, bf16[64,384]{1,0:T(8,128)(2,1)} %k_in.1, bf16[64,384]{1,0:T(8,128)(2,1)} %v_in.1, s32[2,2]{1,0:T(2,128)} %mask_in.1, bf16[2,80,384]{2,1,0:T(8,128)(2,1)} %bitcast.3, bf16[64,2560]{1,0:T(8,128)(2,1)} %res_in.1), custom_call_target="tpu_custom_call" | custom-call | tf_op jit(solution)/shard_map/pallas_call | solution.py:341
  21.4 0.7 %copy.8 = bf16[64,2560]{1,0:T(8,128)(2,1)} copy(bf16[64,2560]{1,0:T(8,128)(2,1)S(1)} %shard_map.64) | data formatting | bytes 655360

commit v3 on v2

--- a/solution.py
+++ b/solution.py
@@ -109,7 +109,7 @@
 def fused_kernel(
     slots, q_in, k_in, v_in, mask_in, w_in, res_in, out_ref,
     qbuf, kv, wt, mask, psend, precv, ssend, srecv,
-    osum, res, blank, load_sem, send_sem, recv_sem,
+    osum, spread_scale, res, blank, load_sem, send_sem, recv_sem,
 ):
     score_scale = 1.0 / math.sqrt(HD)
     g = lax.axis_index("groups")
@@ -126,7 +126,7 @@
     diagonal = {"groups": other, "row": r_chip}
 
     loads = [
-        pltpu.make_async_copy(q_in, qbuf.at[c], load_sem.at[0]),
+        pltpu.make_async_copy(q_in, qbuf.at[0], load_sem.at[0]),
         pltpu.make_async_copy(k_in, kv.at[r, 0], load_sem.at[1]),
         pltpu.make_async_copy(v_in, kv.at[r, 1], load_sem.at[2]),
         pltpu.make_async_copy(w_in, wt.at[r, c], load_sem.at[3]),
@@ -168,62 +168,32 @@
     pair = c + 1 - 2 * lax.rem(c, 2)
     across = lax.rem(c + 2, cols)
     far = lax.rem(pair + 2, cols)
-    targets = [far, across, pair]
-
-    def spread(u, name, direct=True):
-        unit = wt.at[r, u, g]
-        if direct:
-            send(unit, unit, diagonal, name + "_d")
-        send(unit, unit, chip, name + "_x")
-        send(unit, unit, video, name + "_y")
-        send(unit, unit, core, "core_r")
-
-    def relay_y(u, name):
-        wait(name + "_y")
-        unit = wt.at[r, u, other]
-        send(unit, unit, core, "core_r")
-
-    def relay_x(u, name, forward=False):
-        wait(name + "_x")
-        unit = wt.at[r_chip, u, g]
-        send(unit, unit, core, "core_x")
-        if forward:
-            send(unit, unit, video, name + "_d")
-
-    def relay_d(u, name):
-        wait(name + "_d")
-        unit = wt.at[r_chip, u, other]
-        send(unit, unit, core, "core_x")
+    targets = [pair, across, far]
 
     own = qbuf.shape[1]
     key_count = mask.shape[1]
-    query_count = mask.shape[0]
     attended = []
-
-    def attend():
+    home = lax.div(c * own, BLK)
+    first = lax.broadcasted_iota(jnp.int32, (BLK, 2 * own), 1) < own
+
+    def visible(slot, j):
+        block = home if slot < 2 else 1 - home
+        return jnp.where(block == 0, mask[0:1, j : j + 1], mask[1:2, j : j + 1])
+
+    def attend(near, late):
+        pair_rows = [qbuf[near], qbuf[late]]
+        seen = jnp.concatenate(
+            [jnp.where(first, visible(near, j), visible(late, j)) for j in range(key_count)], axis=0
+        )
         for h in range(HEADS):
             lanes = slice(h * HD, (h + 1) * HD)
             key_rows = kv[:, 0, :, lanes].reshape(-1, HD)
             value_rows = kv[:, 1, :, lanes].reshape(-1, HD)
-            query_rows = qbuf[:, :, lanes].reshape(-1, HD)
+            query_rows = jnp.concatenate([rows[:, lanes] for rows in pair_rows], axis=0)
             scores = lax.dot_general(
                 key_rows, query_rows, (((1,), (1,)), ((), ())), preferred_element_type=jnp.float32
             )
-            scores = scores * score_scale
-            seen = jnp.concatenate(
-                [
-                    jnp.concatenate(
-                        [
-                            jnp.broadcast_to(mask[i : i + 1, j : j + 1], (BLK, BLK))
-                            for i in range(query_count)
-                        ],
-                        axis=1,
-                    )
-                    for j in range(key_count)
-                ],
-                axis=0,
-            )
-            scores = jnp.where(seen > 0, scores, -jnp.inf)
+            scores = jnp.where(seen > 0, scores * score_scale, -jnp.inf)
             tile_max = jnp.max(scores, axis=0, keepdims=True)
             weights = jnp.exp(scores - tile_max)
             tile_total = jnp.sum(weights, axis=0, keepdims=True)
@@ -231,48 +201,50 @@
                 weights.astype(jnp.bfloat16), value_rows, (((0,), (0,)), ((), ())),
                 preferred_element_type=jnp.float32,
             )
-            for i in range(cols):
+            for i, slot in enumerate((near, late)):
                 part = slice(i * own, (i + 1) * own)
-                osum[i, :, lanes] = tile_sum[part]
-                psend[i, :, lanes] = tile_sum[part].astype(jnp.bfloat16)
-                ssend[i, h : h + 1, 0:own] = tile_max[:, part]
-                ssend[i, HEADS + h : HEADS + h + 1, 0:own] = tile_total[:, part]
-        for t in targets:
-            send(ssend.at[t], srecv.at[c], {"col": t}, "p")
-            send(psend.at[t], precv.at[c], {"col": t}, "p")
-        precv[c] = psend[c]
-        srecv[c] = ssend[c]
-
-    def merge():
-        wait("p")
-        stats = [srecv[t] for t in range(cols)]
+                ssend[slot, h : h + 1, 0:own] = tile_max[:, part]
+                ssend[slot, HEADS + h : HEADS + h + 1, 0:own] = tile_total[:, part]
+                if slot == 0:
+                    osum[:, lanes] = tile_sum[part]
+                else:
+                    psend[slot - 1, :, lanes] = tile_sum[part].astype(jnp.bfloat16)
+        for slot in (near, late):
+            if slot > 0:
+                send(ssend.at[slot], srecv.at[slot - 1], {"col": targets[slot - 1]}, "s")
+                send(psend.at[slot - 1], precv.at[slot - 1], {"col": targets[slot - 1]}, "p")
+
+    def prepare():
+        wait("s")
+        stats = [ssend[0]] + [srecv[t] for t in range(cols - 1)]
         maxes = [s[0:HEADS, :] for s in stats]
         totals = [s[HEADS : 2 * HEADS, :] for s in stats]
         row_max = functools.reduce(jnp.maximum, maxes)
         factors = [jnp.exp(m - row_max) for m in maxes]
         denom = functools.reduce(jnp.add, [t * f for t, f in zip(totals, factors)])
-        own_factor = jnp.exp(ssend[c, 0:HEADS, :] - row_max)
-        low = osum[c] - psend[c].astype(jnp.float32)
         pad = [jnp.zeros((8 - HEADS, denom.shape[1]), jnp.float32)]
-        table = jnp.concatenate(
-            [x for f in factors + [denom, own_factor] for x in [f] + pad], axis=0
-        )
+        table = jnp.concatenate([x for f in factors for x in [f / denom] + pad], axis=0)
         fill = jnp.zeros((table.shape[1] - table.shape[0], table.shape[1]), jnp.float32)
         table = jnp.concatenate([table, fill], axis=0).T[0:own]
+        for t in range(cols):
+            for h in range(HEADS):
+                column = table[:, 8 * t + h : 8 * t + h + 1]
+                spread_scale[t, h] = jnp.broadcast_to(column, (own, HD))
+        for h in range(HEADS):
+            lanes = slice(h * HD, (h + 1) * HD)
+            osum[:, lanes] = osum[:, lanes] * spread_scale[0, h]
+        loads[5].wait()
+
+    def merge():
+        wait("p")
         heads = []
         for h in range(HEADS):
             lanes = slice(h * HD, (h + 1) * HD)
-            numer = functools.reduce(
-                jnp.add,
-                [
-                    precv[t, :, lanes].astype(jnp.float32) * table[:, 8 * t + h : 8 * t + h + 1]
-                    for t in range(cols)
-                ],
-            )
-            numer += low[:, lanes] * table[:, 8 * cols + 8 + h : 8 * cols + 9 + h]
-            heads.append(numer / table[:, 8 * cols + h : 8 * cols + h + 1])
+            mixed = osum[:, lanes]
+            for t in range(1, cols):
+                mixed += precv[t - 1, :, lanes].astype(jnp.float32) * spread_scale[t, h]
+            heads.append(mixed)
         attended.append(jnp.concatenate(heads, axis=1).astype(jnp.bfloat16))
-        loads[5].wait()
 
     width = cols * 2 * wt.shape[3]
 
@@ -289,8 +261,9 @@
     send(wt.at[r, c, g], wt.at[r, c, g], {"col": across}, "across")
     send(wt.at[r, c, g], wt.at[r, c, g], {"col": pair}, "pair")
     loads[0].wait()
-    for t in targets:
-        send(qbuf.at[c], qbuf.at[c], {"col": t}, "q")
+    send(qbuf.at[0], qbuf.at[3], {"col": far}, "q_far")
+    send(qbuf.at[0], qbuf.at[2], {"col": across}, "q_across")
+    send(qbuf.at[0], qbuf.at[1], {"col": pair}, "q_pair")
     loads[1].wait()
     loads[2].wait()
     send(kv.at[r], kv.at[r], chip, "kv_chip")
@@ -298,31 +271,53 @@
     send(wt.at[r, c], wt.at[r, c], core, "core_r")
     wait("kv_chip")
     send(kv.at[r_chip], kv.at[r_chip], core, "kv_core")
+    send(wt.at[r, c], wt.at[r, c], chip, "own_x")
     wait("across")
     send(wt.at[r, across, g], wt.at[r, across, g], {"col": pair}, "far")
-    spread(across, "across", direct=False)
-    send(wt.at[r, c], wt.at[r, c], chip, "own_x")
+    send(wt.at[r, across, g], wt.at[r, across, g], video, "across_y")
+    send(wt.at[r, across, g], wt.at[r, across, g], chip, "across_x")
+    send(wt.at[r, across, g], wt.at[r, across, g], core, "core_r")
     wait("pair")
-    spread(pair, "pair")
-    wait("q")
+    send(wt.at[r, pair, g], wt.at[r, pair, g], video, "pair_y")
+    send(wt.at[r, pair, g], wt.at[r, pair, g], diagonal, "pair_d")
+    send(wt.at[r, pair, g], wt.at[r, pair, g], chip, "pair_x")
+    send(wt.at[r, pair, g], wt.at[r, pair, g], core, "core_r")
+    wait("q_far")
+    wait("q_across")
     wait("kv_core")
     loads[4].wait()
-    attend()
+    attend(2, 3)
+    wait("q_pair")
+    attend(1, 0)
     wait("far")
-    spread(far, "far")
-    relay_x(across, "across", forward=True)
+    send(wt.at[r, far, g], wt.at[r, far, g], video, "far_y")
+    send(wt.at[r, far, g], wt.at[r, far, g], diagonal, "far_d")
+    send(wt.at[r, far, g], wt.at[r, far, g], chip, "far_x")
+    send(wt.at[r, far, g], wt.at[r, far, g], core, "core_r")
+    wait("across_y")
+    send(wt.at[r, across, other], wt.at[r, across, other], core, "core_r")
+    send(wt.at[r, across, other], wt.at[r, across, other], chip, "across_d")
+    wait("across_x")
+    send(wt.at[r_chip, across, g], wt.at[r_chip, across, g], core, "core_x")
     wait("own_x")
     send(wt.at[r_chip, c], wt.at[r_chip, c], core, "core_x")
-    relay_y(across, "across")
-    relay_x(pair, "pair")
-    relay_y(pair, "pair")
-    relay_d(pair, "pair")
-    relay_x(far, "far")
-    relay_y(far, "far")
-    relay_d(far, "far")
-    relay_d(across, "across")
+    wait("pair_y")
+    send(wt.at[r, pair, other], wt.at[r, pair, other], core, "core_r")
+    wait("pair_x")
+    send(wt.at[r_chip, pair, g], wt.at[r_chip, pair, g], core, "core_x")
+    wait("pair_d")
+    send(wt.at[r_chip, pair, other], wt.at[r_chip, pair, other], core, "core_x")
+    wait("far_y")
+    send(wt.at[r, far, other], wt.at[r, far, other], core, "core_r")
+    prepare()
     merge()
     project(r)
+    wait("far_x")
+    send(wt.at[r_chip, far, g], wt.at[r_chip, far, g], core, "core_x")
+    wait("far_d")
+    send(wt.at[r_chip, far, other], wt.at[r_chip, far, other], core, "core_x")
+    wait("across_d")
+    send(wt.at[r_chip, across, other], wt.at[r_chip, across, other], core, "core_x")
     project(r_chip)
     wait("core_r")
     project(r_core)
@@ -336,7 +331,7 @@
     rows, cols = lax.axis_size("row"), lax.axis_size("col")
     own, width = queries.shape
     depth, part = out_weight.shape
-    slots = 19
+    slots = 22
     any_space = pl.BlockSpec(memory_space=pl.ANY)
     return pl.pallas_call(
         functools.partial(fused_kernel, slots),
@@ -348,11 +343,12 @@
             pltpu.VMEM((rows, 2, own, width), jnp.bfloat16),
             pltpu.VMEM((rows, cols, 2, part // 2, depth), jnp.bfloat16),
             pltpu.VMEM(block_mask.shape, jnp.int32),
-            pltpu.VMEM((cols, own, width), jnp.bfloat16),
-            pltpu.VMEM((cols, own, width), jnp.bfloat16),
+            pltpu.VMEM((cols - 1, own, width), jnp.bfloat16),
+            pltpu.VMEM((cols - 1, own, width), jnp.bfloat16),
             pltpu.VMEM((cols, 8, BLK), jnp.float32),
-            pltpu.VMEM((cols, 8, BLK), jnp.float32),
-            pltpu.VMEM((cols, own, width), jnp.float32),
+            pltpu.VMEM((cols - 1, 8, BLK), jnp.float32),
+            pltpu.VMEM((own, width), jnp.float32),
+            pltpu.VMEM((cols, HEADS, own, HD), jnp.float32),
             pltpu.VMEM(residual.shape, jnp.bfloat16),
             pltpu.VMEM((rows * cols * 2 * part * depth // BLK, BLK), jnp.bfloat16),
             pltpu.SemaphoreType.DMA((6,)),

time: 22.6 us -> 21.9 us (0.969); the launches traced: 22.2 us -> 21.8 us
  Pallas kernels: 21.4 us -> 21.1 us
    pallas_call x1, Pallas kernels: 21.4 us -> 21.1 us  [fused(): pl.pallas_call(functools.partial(fused_kernel, slots), out_shape=pltpu.VM...]
where the time goes in v3:
time: 21.9 us; the launch traced here: 21.8 us
  Pallas kernels  21.1 us (96%)
  local copies, waits for them, and re-layouts  0.73 us (3%)
    pallas_call x1, Pallas kernels, fused(): pl.pallas_call(functools.partial(fused_kernel, slots), out_shape=pltpu.VM...  21.1 us
    unnamed x1, local copies, waits for them, and re-layouts  0.73 us

profile of v3, /device:TPU:1, one launch (start us, length us, event | category | flops | bytes accessed | tf_op | source)
XLA Modules:
  0.0 21.8 jit_solution(2702004779956074312)
XLA Ops:
  0.0 21.1 %shard_map.64 = bf16[64,2560]{1,0:T(8,128)(2,1)S(1)} custom-call(bf16[64,384]{1,0:T(8,128)(2,1)} %q_in.1, bf16[64,384]{1,0:T(8,128)(2,1)} %k_in.1, bf16[64,384]{1,0:T(8,128)(2,1)} %v_in.1, s32[2,2]{1,0:T(2,128)} %mask_in.1, bf16[2,80,384]{2,1,0:T(8,128)(2,1)} %bitcast.3, bf16[64,2560]{1,0:T(8,128)(2,1)} %res_in.1), custom_call_target="tpu_custom_call" | custom-call | tf_op jit(solution)/shard_map/pallas_call | solution.py:336
  21.1 0.7 %copy.8 = bf16[64,2560]{1,0:T(8,128)(2,1)} copy(bf16[64,2560]{1,0:T(8,128)(2,1)S(1)} %shard_map.64) | data formatting | bytes 655360

commit v4 on v3

--- a/solution.py
+++ b/solution.py
@@ -272,21 +272,23 @@
     wait("kv_chip")
     send(kv.at[r_chip], kv.at[r_chip], core, "kv_core")
     send(wt.at[r, c], wt.at[r, c], chip, "own_x")
+    wait("pair")
+    send(wt.at[r, pair, g], wt.at[r, pair, g], video, "pair_y")
+    send(wt.at[r, pair, g], wt.at[r, pair, g], chip, "pair_x")
+    send(wt.at[r, pair, g], wt.at[r, pair, g], core, "core_r")
     wait("across")
     send(wt.at[r, across, g], wt.at[r, across, g], {"col": pair}, "far")
+    send(wt.at[r, across, g], wt.at[r, across, g], chip, "across_x")
     send(wt.at[r, across, g], wt.at[r, across, g], video, "across_y")
-    send(wt.at[r, across, g], wt.at[r, across, g], chip, "across_x")
     send(wt.at[r, across, g], wt.at[r, across, g], core, "core_r")
-    wait("pair")
-    send(wt.at[r, pair, g], wt.at[r, pair, g], video, "pair_y")
-    send(wt.at[r, pair, g], wt.at[r, pair, g], diagonal, "pair_d")
-    send(wt.at[r, pair, g], wt.at[r, pair, g], chip, "pair_x")
-    send(wt.at[r, pair, g], wt.at[r, pair, g], core, "core_r")
     wait("q_far")
     wait("q_across")
     wait("kv_core")
     loads[4].wait()
     attend(2, 3)
+    wait("pair_y")
+    send(wt.at[r, pair, other], wt.at[r, pair, other], core, "core_r")
+    send(wt.at[r, pair, other], wt.at[r, pair, other], chip, "pair_d")
     wait("q_pair")
     attend(1, 0)
     wait("far")
@@ -294,15 +296,13 @@
     send(wt.at[r, far, g], wt.at[r, far, g], diagonal, "far_d")
     send(wt.at[r, far, g], wt.at[r, far, g], chip, "far_x")
     send(wt.at[r, far, g], wt.at[r, far, g], core, "core_r")
+    wait("across_x")
+    send(wt.at[r_chip, across, g], wt.at[r_chip, across, g], core, "core_x")
+    send(wt.at[r_chip, across, g], wt.at[r_chip, across, g], video, "across_d")
+    wait("own_x")
+    send(wt.at[r_chip, c], wt.at[r_chip, c], core, "core_x")
     wait("across_y")
     send(wt.at[r, across, other], wt.at[r, across, other], core, "core_r")
-    send(wt.at[r, across, other], wt.at[r, across, other], chip, "across_d")
-    wait("across_x")
-    send(wt.at[r_chip, across, g], wt.at[r_chip, across, g], core, "core_x")
-    wait("own_x")
-    send(wt.at[r_chip, c], wt.at[r_chip, c], core, "core_x")
-    wait("pair_y")
-    send(wt.at[r, pair, other], wt.at[r, pair, other], core, "core_r")
     wait("pair_x")
     send(wt.at[r_chip, pair, g], wt.at[r_chip, pair, g], core, "core_x")
     wait("pair_d")

time: 21.9 us -> 21.6 us (0.986); the launches traced: 21.8 us -> 21.3 us
  Pallas kernels: 21.1 us -> 20.5 us
    pallas_call x1, Pallas kernels: 21.1 us -> 20.5 us  [fused(): pl.pallas_call(functools.partial(fused_kernel, slots), out_shape=pltpu.VM...]
where the time goes in v4:
time: 21.6 us; the launch traced here: 21.3 us
  Pallas kernels  20.5 us (95%)
  local copies, waits for them, and re-layouts  0.73 us (3%)
    pallas_call x1, Pallas kernels, fused(): pl.pallas_call(functools.partial(fused_kernel, slots), out_shape=pltpu.VM...  20.5 us
    unnamed x1, local copies, waits for them, and re-layouts  0.73 us

profile of v4, /device:TPU:1, one launch (start us, length us, event | category | flops | bytes accessed | tf_op | source)
XLA Modules:
  0.0 21.3 jit_solution(16307940362998887967)
XLA Ops:
  0.0 20.5 %shard_map.64 = bf16[64,2560]{1,0:T(8,128)(2,1)S(1)} custom-call(bf16[64,384]{1,0:T(8,128)(2,1)} %q_in.1, bf16[64,384]{1,0:T(8,128)(2,1)} %k_in.1, bf16[64,384]{1,0:T(8,128)(2,1)} %v_in.1, s32[2,2]{1,0:T(2,128)} %mask_in.1, bf16[2,80,384]{2,1,0:T(8,128)(2,1)} %bitcast.3, bf16[64,2560]{1,0:T(8,128)(2,1)} %res_in.1), custom_call_target="tpu_custom_call" | custom-call | tf_op jit(solution)/shard_map/pallas_call | solution.py:336
  20.5 0.7 %copy.8 = bf16[64,2560]{1,0:T(8,128)(2,1)} copy(bf16[64,2560]{1,0:T(8,128)(2,1)S(1)} %shard_map.64) | data formatting | bytes 655360

commit v5 on v4

--- a/solution.py
+++ b/solution.py
@@ -137,7 +137,7 @@
         load.start()
 
     barrier = pltpu.get_barrier_semaphore()
-    peers = [{"col": lax.rem(c + j, cols)} for j in range(1, cols)] + [chip, core, video, diagonal]
+    peers = [{"col": lax.rem(c + j, cols)} for j in range(1, cols)] + [chip, core, video]
     for peer in peers:
         pl.semaphore_signal(barrier, inc=1, device_id=peer, device_id_type=MESH)
     pl.semaphore_wait(barrier, len(peers))
@@ -269,9 +269,9 @@
     send(kv.at[r], kv.at[r], chip, "kv_chip")
     send(kv.at[r], kv.at[r], core, "kv_core")
     send(wt.at[r, c], wt.at[r, c], core, "core_r")
+    send(wt.at[r, c, g], wt.at[r, c, g], chip, "own_x")
     wait("kv_chip")
     send(kv.at[r_chip], kv.at[r_chip], core, "kv_core")
-    send(wt.at[r, c], wt.at[r, c], chip, "own_x")
     wait("pair")
     send(wt.at[r, pair, g], wt.at[r, pair, g], video, "pair_y")
     send(wt.at[r, pair, g], wt.at[r, pair, g], chip, "pair_x")
@@ -281,6 +281,9 @@
     send(wt.at[r, across, g], wt.at[r, across, g], chip, "across_x")
     send(wt.at[r, across, g], wt.at[r, across, g], video, "across_y")
     send(wt.at[r, across, g], wt.at[r, across, g], core, "core_r")
+    wait("own_x")
+    send(wt.at[r_chip, c, g], wt.at[r_chip, c, g], core, "core_x")
+    send(wt.at[r_chip, c, g], wt.at[r_chip, c, g], video, "own_y")
     wait("q_far")
     wait("q_across")
     wait("kv_core")
@@ -299,10 +302,10 @@
     wait("across_x")
     send(wt.at[r_chip, across, g], wt.at[r_chip, across, g], core, "core_x")
     send(wt.at[r_chip, across, g], wt.at[r_chip, across, g], video, "across_d")
-    wait("own_x")
-    send(wt.at[r_chip, c], wt.at[r_chip, c], core, "core_x")
     wait("across_y")
     send(wt.at[r, across, other], wt.at[r, across, other], core, "core_r")
+    wait("own_y")
+    send(wt.at[r_chip, c, other], wt.at[r_chip, c, other], core, "core_x")
     wait("pair_x")
     send(wt.at[r_chip, pair, g], wt.at[r_chip, pair, g], core, "core_x")
     wait("pair_d")
@@ -331,7 +334,7 @@
     rows, cols = lax.axis_size("row"), lax.axis_size("col")
     own, width = queries.shape
     depth, part = out_weight.shape
-    slots = 22
+    slots = 23
     any_space = pl.BlockSpec(memory_space=pl.ANY)
     return pl.pallas_call(
         functools.partial(fused_kernel, slots),

time: 21.6 us -> 21.4 us (level)
  no operation moved by 1% of the time
where the time goes in v5:
time: 21.4 us; the launch traced here: 21.3 us
  Pallas kernels  20.5 us (96%)
  local copies, waits for them, and re-layouts  0.73 us (3%)
    pallas_call x1, Pallas kernels, fused(): pl.pallas_call(functools.partial(fused_kernel, slots), out_shape=pltpu.VM...  20.5 us
    unnamed x1, local copies, waits for them, and re-layouts  0.73 us

profile of v5, /device:TPU:1, one launch (start us, length us, event | category | flops | bytes accessed | tf_op | source)
XLA Modules:
  0.0 21.3 jit_solution(1746805166697966987)
XLA Ops:
  0.0 20.5 %shard_map.64 = bf16[64,2560]{1,0:T(8,128)(2,1)S(1)} custom-call(bf16[64,384]{1,0:T(8,128)(2,1)} %q_in.1, bf16[64,384]{1,0:T(8,128)(2,1)} %k_in.1, bf16[64,384]{1,0:T(8,128)(2,1)} %v_in.1, s32[2,2]{1,0:T(2,128)} %mask_in.1, bf16[2,80,384]{2,1,0:T(8,128)(2,1)} %bitcast.3, bf16[64,2560]{1,0:T(8,128)(2,1)} %res_in.1), custom_call_target="tpu_custom_call" | custom-call | tf_op jit(solution)/shard_map/pallas_call | solution.py:339
  20.5 0.7 %copy.8 = bf16[64,2560]{1,0:T(8,128)(2,1)} copy(bf16[64,2560]{1,0:T(8,128)(2,1)S(1)} %shard_map.64) | data formatting | bytes 655360

commit v6 on v5

--- a/solution.py
+++ b/solution.py
@@ -133,13 +133,14 @@
         pltpu.make_async_copy(mask_in, mask, load_sem.at[4]),
         pltpu.make_async_copy(res_in, res, load_sem.at[5]),
     ]
-    for load in loads:
-        load.start()
-
     barrier = pltpu.get_barrier_semaphore()
     peers = [{"col": lax.rem(c + j, cols)} for j in range(1, cols)] + [chip, core, video]
     for peer in peers:
         pl.semaphore_signal(barrier, inc=1, device_id=peer, device_id_type=MESH)
+
+    for load in loads:
+        load.start()
+
     pl.semaphore_wait(barrier, len(peers))
 
     bytes_of = {}

time: 21.4 us -> 21.4 us (level)
  no operation moved by 1% of the time
where the time goes in v6:
time: 21.4 us; the launch traced here: 21.3 us
  Pallas kernels  20.5 us (96%)
  local copies, waits for them, and re-layouts  0.73 us (3%)
    pallas_call x1, Pallas kernels, fused(): pl.pallas_call(functools.partial(fused_kernel, slots), out_shape=pltpu.VM...  20.5 us
    unnamed x1, local copies, waits for them, and re-layouts  0.73 us

profile of v6, /device:TPU:1, one launch (start us, length us, event | category | flops | bytes accessed | tf_op | source)
XLA Modules:
  0.0 21.3 jit_solution(17330920551795434062)
XLA Ops:
  0.0 20.5 %shard_map.64 = bf16[64,2560]{1,0:T(8,128)(2,1)S(1)} custom-call(bf16[64,384]{1,0:T(8,128)(2,1)} %q_in.1, bf16[64,384]{1,0:T(8,128)(2,1)} %k_in.1, bf16[64,384]{1,0:T(8,128)(2,1)} %v_in.1, s32[2,2]{1,0:T(2,128)} %mask_in.1, bf16[2,80,384]{2,1,0:T(8,128)(2,1)} %bitcast.3, bf16[64,2560]{1,0:T(8,128)(2,1)} %res_in.1), custom_call_target="tpu_custom_call" | custom-call | tf_op jit(solution)/shard_map/pallas_call | solution.py:340
  20.5 0.7 %copy.8 = bf16[64,2560]{1,0:T(8,128)(2,1)} copy(bf16[64,2560]{1,0:T(8,128)(2,1)S(1)} %shard_map.64) | data formatting | bytes 655360
